TPU v7x, 32 devices: a whole 2x2x4 slice. The times are simulated.
32 devices in a mesh: groups: 2 (over y), section: 4 (over z), head: 4 (over x, core).
Axes of the slice: x: 2, y: 2, z: 4, core: 2. Of those that a mesh axis runs over, the one named last changes fastest.
Arguments:
- rising: bfloat16 [8, 128, 1024], P(('groups', 'section')), parts along dimension 0, may hold values from -24 to 24
- falling: bfloat16 [8, 128, 1024], P(('groups', 'section')), parts along dimension 0, may hold values from -6 to 6
- stash: bfloat16 [8, 3, 128, 1024], P(('groups', 'section')), parts along dimension 0, may hold values from -24 to 24
- queue: bfloat16 [12, 128, 1024], P('groups'), parts along dimension 0, may hold values from -24 to 24
- order: int32 [12], P('groups'), parts along dimension 0, may hold values from 0 to 5, each once
- buckets: int32 [128, 128], replicated, may hold values from 0 to 31, as said below
- bias_table: float32 [4, 32, 64], P('section', None, 'head'), may hold values from -3 to 260
- gain: float32 [4, 1024], P('section'), may hold values from 0.1 to 1.9
- w_qkv: bfloat16 [4, 1024, 64, 3, 128], P('section', None, 'head'), may hold values from -0.1875 to 0.1875
- w_out: bfloat16 [4, 64, 128, 1024], P('section', 'head'), may hold values from -0.0625 to 0.0625
Outputs:
- rising_out: bfloat16 [8, 128, 1024], P(('groups', 'section')), parts along dimension 0
- falling_out: bfloat16 [8, 128, 1024], P(('groups', 'section')), parts along dimension 0
- table_grad: float32 [8, 32, 64], P(('groups', 'section'), None, 'head'), parts along dimension 0
There are 2 independent parts, one for each index of `groups`. A program takes and returns all parts, laid end to end along the dimension named above; an argument that names none is the same for every part. Nothing has to cross between parts.
Inputs may be any that keep to these rules, and one draw needn't show every extreme that they name: `order`: a permutation of 0 to 5. T5's bidirectional bucket of the key's position minus the query's, 32 buckets, distances of 128 or more in the outermost; positions rise by 1 to 4 from token to token, with one jump of 128 or more.
All inputs are finite; a program needn't handle non-finite values.
Results may differ from a plain program's by a relative error of at most 0.019.
Values may be sent and summed in bfloat16 or wider, within the bound.
A program may use at most 128 MiB of HBM per device.

v0:
```python
import functools

import jax
import jax.numpy as jnp
from jax import lax
from jax.experimental import pallas as pl
from jax.experimental.pallas import tpu as pltpu
from jax.sharding import PartitionSpec as P

EPSILON = 1e-06
MESH = pl.DeviceIdType.MESH
NN = (((1,), (0,)), ((), ()))
NT = (((1,), (1,)), ((), ()))
TN = (((0,), (0,)), ((), ()))


def mm(a, b, dims):
    return lax.dot_general(a, b, dims, preferred_element_type=jnp.float32)


def inverse_rms(x):
    return lax.rsqrt(jnp.mean(x * x, axis=-1, keepdims=True) + EPSILON)


def probabilities(q, k, bias, scale):
    scores = mm(q, k, NT) * scale + bias
    top = jnp.max(scores, axis=-1, keepdims=True)
    raised = jnp.exp(scores - top)
    return raised / jnp.sum(raised, axis=-1, keepdims=True)


def wave_kernel(
    ticks, steps, pair, head_dim, chips, sections,
    order, rising, falling, stash, queue, gain, bias, w_hbm, wo_hbm,
    out_up, out_down, total,
    w, wo, normed, flat_down, acc, cur, part, near, away, far, share,
    w_sem, near_send, near_recv, far_send, far_recv,
    lift_send, lift_recv, gather_send, gather_recv, pass_send, pass_recv,
):
    tick, phase, step = pl.program_id(0), pl.program_id(1), pl.program_id(2)
    section = lax.axis_index("section")
    head = lax.axis_index("head")
    chip, core = head // 2, lax.rem(head, 2)
    twin = chip * 2 + (1 - core)
    rows, width = flat_down.shape
    scale = head_dim ** (-0.5)
    span = pair * head_dim

    def peer(k):
        return lax.rem(chip + k, chips)

    def remote(src, dst, send, recv, target):
        return pltpu.make_async_remote_copy(
            src_ref=src, dst_ref=dst, send_sem=send, recv_sem=recv,
            device_id=target, device_id_type=MESH,
        )

    def flat(x):
        return x.astype(jnp.float32).reshape(rows, width)

    def load(j, c):
        if c < 3:
            source = w_hbm.at[:, pl.ds((c * steps + j) * span, span)]
            return pltpu.make_async_copy(source, w.at[j, c], w_sem.at[j, c])
        return pltpu.make_async_copy(wo_hbm.at[pl.ds(j * span, span)], wo.at[j], w_sem.at[j, 3])

    def near_copy(which, t, k):
        return remote(
            part.at[which, t, peer(k), 1 - core], near.at[which, t, k],
            near_send.at[which, t, k], near_recv.at[which, t, k], {"head": twin},
        )

    def far_copy(which, t, k):
        return remote(
            away.at[which, t, k - 1], far.at[which, t, k - 1],
            far_send.at[which, t, k - 1], far_recv.at[which, t, k - 1],
            {"head": peer(k) * 2 + core},
        )

    def lift_copy(which, t, target):
        return remote(
            share.at[which, t], cur.at[which, t + 1, chip, core],
            lift_send.at[which, t], lift_recv.at[which, t], {"section": target},
        )

    def gather_copy(which, t, k):
        rows_here = cur.at[which, t + 1, chip, core]
        return remote(
            rows_here, rows_here,
            gather_send.at[which, t, k - 1], gather_recv.at[which, t, k - 1],
            {"head": peer(k) * 2 + core},
        )

    def pass_copy(which, t, k):
        rows_here = cur.at[which, t + 1, lax.rem(chip - k + chips, chips), core]
        return remote(
            rows_here, rows_here,
            pass_send.at[which, t, k], pass_recv.at[which, t, k], {"head": twin},
        )

    def begin(which, t):
        part[which, t] = acc[...].reshape(part.shape[2:]).astype(jnp.bfloat16)
        for k in list(range(1, chips)) + [0]:
            near_copy(which, t, k).start()

    def fold(which, t):
        for k in range(1, chips):
            near_copy(which, t, k).wait_recv()
            away[which, t, k - 1] = (
                part[which, t, peer(k), core].astype(jnp.float32)
                + near[which, t, k].astype(jnp.float32)
            ).astype(jnp.bfloat16)
            far_copy(which, t, k).start()

    def ends(which):
        if which == 0:
            return section < sections - 1, section + 1, section > 0, section - 1
        return section > 0, section - 1, section < sections - 1, section + 1

    def finish(which, t):
        near_copy(which, t, 0).wait_recv()
        own = part[which, t, chip, core].astype(jnp.float32) + near[which, t, 0].astype(
            jnp.float32
        )
        for k in range(1, chips):
            far_copy(which, t, k).wait_recv()
            own = own + far[which, t, k - 1].astype(jnp.float32)
        before = cur[which, t, chip, core].astype(jnp.float32)
        if which == 0:
            result = before + own
        else:
            x = stash[t, chip, core].astype(jnp.float32)
            inverse = inverse_rms(x)
            cubed = inverse * inverse * inverse
            weighted = gain[...] * own
            result = (
                before
                + inverse * weighted
                - x * cubed * jnp.mean(x * weighted, axis=-1, keepdims=True)
            )
        share[which, t] = result.astype(jnp.bfloat16)
        sends, target, receives, _ = ends(which)

        @pl.when(t == ticks - 1)
        def _():
            cur[which, t + 1, chip, core] = result.astype(jnp.bfloat16)

        @pl.when((t < ticks - 1) & sends)
        def _():
            lift_copy(which, t, target).start()

        @pl.when((t < ticks - 1) & jnp.logical_not(receives))
        def _():
            if which == 0:
                cur[which, t + 1, chip, core] = queue[order[t], chip, core]
            else:
                cur[which, t + 1, chip, core] = share[0, t]

    def spread(which, t):
        sends, target, receives, source = ends(which)

        @pl.when((t < ticks - 1) & receives)
        def _():
            lift_copy(which, t, source).wait_recv()

        for k in range(1, chips):
            gather_copy(which, t, k).start()
        pass_copy(which, t, 0).start()

    def relay(which, t):
        for k in range(1, chips):
            gather_copy(which, t, k).wait_recv()
            pass_copy(which, t, k).start()

    def settle(which, t):
        sends, target, receives, source = ends(which)
        for k in range(chips):
            pass_copy(which, t, k).wait_recv()
        for k in range(chips):
            near_copy(which, t, k).wait_send()
            pass_copy(which, t, k).wait_send()
        for k in range(1, chips):
            far_copy(which, t, k).wait_send()
            gather_copy(which, t, k).wait_send()

        @pl.when((t < ticks - 1) & sends)
        def _():
            lift_copy(which, t, target).wait_send()

    stages = ((fold, 2), (finish, 4), (spread, 6), (relay, 7))

    def normalize(x):
        normed[...] = (x * inverse_rms(x) * gain[...]).astype(jnp.bfloat16)

    @pl.when((tick == 0) & (phase == 0) & (step == 0))
    def _():
        for j in range(steps):
            for c in range(4):
                load(j, c).start()
        barrier = pltpu.get_barrier_semaphore()
        greeted = [twin] + [peer(k) * 2 + core for k in range(1, chips)]
        for other in greeted:
            pl.semaphore_signal(barrier, inc=1, device_id={"head": other}, device_id_type=MESH)

        @pl.when(section > 0)
        def _():
            pl.semaphore_signal(
                barrier, inc=1, device_id={"section": section - 1}, device_id_type=MESH
            )

        @pl.when(section < sections - 1)
        def _():
            pl.semaphore_signal(
                barrier, inc=1, device_id={"section": section + 1}, device_id_type=MESH
            )

        cur[0, 0] = rising[...]
        cur[1, 0] = falling[...]
        flat_down[...] = flat(falling[...]).astype(jnp.bfloat16)
        total[...] = jnp.zeros_like(total)
        pl.semaphore_wait(
            barrier,
            len(greeted)
            + (section > 0).astype(jnp.int32)
            + (section < sections - 1).astype(jnp.int32),
        )

    @pl.when(phase == 0)
    def _():
        @pl.when(step == 0)
        def _():
            @pl.when(tick > 0)
            def _():
                settle(0, tick - 1)

            normalize(flat(cur[0, tick]))
            acc[...] = jnp.zeros_like(acc)

        @pl.when(tick == 0)
        def _():
            for c in range(4):
                load(step, c).wait()

        for stage, at in stages:
            @pl.when((tick > 0) & (step == at * steps // 8))
            def _(stage=stage):
                stage(1, tick - 1)

        qkv = [mm(normed[...], w[step, c], NN).astype(jnp.bfloat16) for c in range(3)]
        attended = []
        for h in range(pair):
            q, k, v = (a[:, h * head_dim : (h + 1) * head_dim] for a in qkv)
            probs = probabilities(q, k, bias[step * pair + h], scale).astype(jnp.bfloat16)
            attended.append(mm(probs, v, NN).astype(jnp.bfloat16))
        acc[...] += mm(jnp.concatenate(attended, axis=1), wo[step], NN)

        @pl.when(step == steps - 1)
        def _():
            begin(0, tick)

    @pl.when(phase == 1)
    def _():
        @pl.when(step == 0)
        def _():
            @pl.when(tick > 0)
            def _():
                settle(1, tick - 1)
                flat_down[...] = flat(cur[1, tick]).astype(jnp.bfloat16)

            normalize(flat(stash[tick]))
            acc[...] = jnp.zeros_like(acc)

        for stage, at in stages:
            @pl.when(step == at * steps // 8)
            def _(stage=stage):
                stage(0, tick)

        qkv = [mm(normed[...], w[step, c], NN).astype(jnp.bfloat16) for c in range(3)]
        grad_flat = mm(flat_down[...], wo[step], NT).astype(jnp.bfloat16)
        stacked = []
        for h in range(pair):
            columns = slice(h * head_dim, (h + 1) * head_dim)
            q, k, v = (a[:, columns] for a in qkv)
            g = grad_flat[:, columns]
            probs = probabilities(q, k, bias[step * pair + h], scale)
            grad_probs = mm(g, v, NT)
            grad_value = mm(probs.astype(jnp.bfloat16), g, TN).astype(jnp.bfloat16)
            grad_scores = probs * (
                grad_probs - jnp.sum(probs * grad_probs, axis=-1, keepdims=True)
            )
            half = grad_scores.astype(jnp.bfloat16)
            grad_query = (mm(half, k, NN) * scale).astype(jnp.bfloat16)
            grad_key = (mm(half, q, TN) * scale).astype(jnp.bfloat16)
            stacked.append((grad_query, grad_key, grad_value))
            total[step * pair + h] += grad_scores
        back = [
            mm(jnp.concatenate(g, axis=1), w[step, c], NT) for c, g in enumerate(zip(*stacked))
        ]
        acc[...] += back[0] + back[1] + back[2]

        @pl.when(step == steps - 1)
        def _():
            begin(1, tick)

    @pl.when((tick == ticks - 1) & (phase == 1) & (step == steps - 1))
    def _():
        last = ticks - 1
        settle(0, last)
        for stage, _at in stages:
            stage(1, last)
        out_up[...] = cur[0, ticks]
        settle(1, last)
        out_down[...] = cur[1, ticks]


def per_device(rising, falling, stash, queue, order, buckets, bias_table, gain, w_qkv, w_out):
    sections = lax.axis_size("section")
    head_count = lax.axis_size("head")
    ticks = stash.shape[1]
    rows, width = rising.shape[1:]
    heads, head_dim = w_qkv.shape[2], w_qkv.shape[4]
    chips, part_rows = head_count // 2, rows // head_count
    pair = 2 if heads % 2 == 0 else 1
    steps, span = heads // pair, pair * head_dim
    others = max(chips - 1, 1)
    w_in = jnp.swapaxes(w_qkv[0], 1, 2).reshape(width, 3 * heads * head_dim)
    w_back = w_out[0].reshape(heads * head_dim, width)
    bucket_ids = jnp.arange(bias_table.shape[1], dtype=jnp.int32)
    onehot = (buckets[None, :, :] == bucket_ids[:, None, None]).astype(jnp.float32)
    biases = jnp.einsum("bij,bh->hij", onehot, bias_table[0], precision=lax.Precision.HIGHEST)
    split = lambda a: a.reshape(a.shape[:-2] + (chips, 2, part_rows, width))
    vmem = pl.BlockSpec(memory_space=pltpu.VMEM)
    anywhere = pl.BlockSpec(memory_space=pl.ANY)
    tile = (part_rows, width)
    bf16 = lambda *shape: pltpu.VMEM(shape, jnp.bfloat16)
    dma = lambda *shape: pltpu.SemaphoreType.DMA(shape)
    up, down, total = pl.pallas_call(
        functools.partial(wave_kernel, ticks, steps, pair, head_dim, chips, sections),
        grid=(ticks, 2, steps),
        in_specs=[pl.BlockSpec(memory_space=pltpu.SMEM)] + [vmem] * 6 + [anywhere] * 2,
        out_specs=[vmem] * 3,
        out_shape=[
            jax.ShapeDtypeStruct((chips, 2) + tile, jnp.bfloat16),
            jax.ShapeDtypeStruct((chips, 2) + tile, jnp.bfloat16),
            jax.ShapeDtypeStruct((heads, rows, rows), jnp.float32),
        ],
        scratch_shapes=[
            bf16(steps, 3, width, span),
            bf16(steps, span, width),
            bf16(rows, width),
            bf16(rows, width),
            pltpu.VMEM((rows, width), jnp.float32),
            bf16(2, ticks + 1, chips, 2, *tile),
            bf16(2, ticks, chips, 2, *tile),
            bf16(2, ticks, chips, *tile),
            bf16(2, ticks, others, *tile),
            bf16(2, ticks, others, *tile),
            bf16(2, ticks, *tile),
            dma(steps, 4),
            dma(2, ticks, chips), dma(2, ticks, chips),
            dma(2, ticks, others), dma(2, ticks, others),
            dma(2, ticks), dma(2, ticks),
            dma(2, ticks, others), dma(2, ticks, others),
            dma(2, ticks, chips), dma(2, ticks, chips),
        ],
        compiler_params=pltpu.CompilerParams(
            collective_id=0, has_side_effects=True, vmem_limit_bytes=58 << 20
        ),
    )(
        order, split(rising[0]), split(falling[0]), split(stash[0]), split(queue), gain,
        biases, w_in, w_back,
    )
    table_grad = jnp.einsum("bij,hij->bh", onehot, total, precision=lax.Precision.HIGHEST)
    return (up.reshape(1, rows, width), down.reshape(1, rows, width), table_grad[None])


def solution(mesh):
    return jax.shard_map(
        per_device,
        mesh=mesh,
        in_specs=(
            P(("groups", "section"), None, None),
            P(("groups", "section"), None, None),
            P(("groups", "section"), None, None, None),
            P("groups", None, None),
            P("groups"),
            P(),
            P("section", None, "head"),
            P("section", None),
            P("section", None, "head", None, None),
            P("section", "head", None, None),
        ),
        out_specs=(
            P(("groups", "section"), None, None),
            P(("groups", "section"), None, None),
            P(("groups", "section"), None, "head"),
        ),
        check_vma=False,
    )
```

profile of v0, /device:TPU:0, one launch (start us, length us, event | category | flops | bytes accessed | tf_op | source)
XLA Modules:
  0.0 136.3 jit_solution(14741138591056439247)
XLA Ops:
  0.6 0.0 copy-start
  0.6 0.7 copy-done
  1.3 1.6 %fusion.1 = f32[128,128,16]{1,2,0:T(8,128)S(1)} fusion(s32[128,128]{1,0:T(8,128)} %param.15, f32[1,32,16]{1,2,0:T(8,128)S(1)} %copy-done), kind=kOutput, calls=%fused_computation.3 | convolution fusion | flops 101187584 | bytes 1116160 | tf_op jit(solution)/shard_map/bij,bh->hij/dot_general | solution.py:330
  2.9 1.4 copy.21
  4.3 13.4 %copy.20 = bf16[128,8,48,128]{3,1,2,0:T(8,128)(2,1)} copy(bf16[128,8,48,128]{3,2,1,0:T(8,128)(2,1)} %bitcast.26) | data formatting | bytes 25165824
  17.7 0.0 copy-start.1
  17.7 111.8 %shard_map.121 = (bf16[2,2,32,1024]{3,2,1,0:T(8,128)(2,1)}, bf16[2,2,32,1024]{3,2,1,0:T(8,128)(2,1)}, f32[16,128,128]{2,1,0:T(8,128)}) custom-call(s32[6]{0:T(128)} %order.1, bf16[2,2,32,1024]{3,2,1,0:T(8,128)(2,1)} %bitcast.31, bf16[2,2,32,1024]{3,2,1,0:T(8,128)(2,1)} %bitcast.32, bf16[3,2,2,32,1024]{4,3,2,1,0:T(8,128)(2,1)} %bitcast.30, ...), custom_call_target="tpu_custom_call" | custom-call | tf_op jit(solution)/shard_map/pallas_call | solution.py:337
  129.6 0.0 copy-done.1
  129.6 3.4 %fusion.2 = f32[1,32,16]{1,2,0:T(8,128)} fusion(f32[16,128,128]{2,1,0:T(8,128)} %get-tuple-element.8, s32[128,128]{1,0:T(8,128)S(1)} %copy-done.1), kind=kOutput, calls=%fused_computation.4 | convolution fusion | flops 101187584 | bytes 1116160 | tf_op jit(solution)/shard_map/bij,hij->bh/dot_general | solution.py:373
  132.9 1.7 %copy.24 = bf16[1,128,1024]{2,1,0:T(8,128)(2,1)} copy(bf16[1,128,1024]{2,1,0:T(8,128)(2,1)} %bitcast.34) | data formatting | bytes 524288
  134.6 1.7 %copy.25 = bf16[1,128,1024]{2,1,0:T(8,128)(2,1)} copy(bf16[1,128,1024]{2,1,0:T(8,128)(2,1)} %bitcast.33) | data formatting | bytes 524288
Async XLA Ops:
  0.6 0.7 copy-start
  17.7 111.9 %copy-start.1 = (s32[128,128]{1,0:T(8,128)S(1)}, s32[128,128]{1,0:T(8,128)}, u32[]{:S(2)}) copy-start(s32[128,128]{1,0:T(8,128)} %param.15) | copy-start | bytes 196612
where the time goes:
time: 137 us; the launch traced here: 136 us
  Pallas kernels  112 us (82%)
  local copies, waits for them, and re-layouts  18.8 us (14%)
  matrix products  4.95 us (4%)
    pallas_call x1, Pallas kernels, per_device(): pl.pallas_call(functools.partial(wave_kernel, ticks, steps, pair, head_di...  112 us
    unnamed x7, local copies, waits for them, and re-layouts  17.5 us
    dot_general x1, matrix products, per_device(): jnp.einsum('bij,hij->bh', onehot, total, precision=lax.Precision.HIGHEST)  3.37 us

commit v1 on v0

v1 whole, which is shorter than its diff:
```python
import functools

import jax
import jax.numpy as jnp
from jax import lax
from jax.experimental import pallas as pl
from jax.experimental.pallas import tpu as pltpu
from jax.sharding import PartitionSpec as P

EPSILON = 1e-06
MESH = pl.DeviceIdType.MESH
NN = (((1,), (0,)), ((), ()))
NT = (((1,), (1,)), ((), ()))
TN = (((0,), (0,)), ((), ()))


def mm(a, b, dims):
    return lax.dot_general(a, b, dims, preferred_element_type=jnp.float32)


def inverse_rms(x):
    return lax.rsqrt(jnp.mean(x * x, axis=-1, keepdims=True) + EPSILON)


def probabilities(q, k, bias, scale):
    scores = mm(q, k, NT) * scale + bias
    top = jnp.max(scores, axis=-1, keepdims=True)
    raised = jnp.exp(scores - top)
    return raised / jnp.sum(raised, axis=-1, keepdims=True)


def wave_kernel(
    ticks, steps, pair, head_dim, chips, sections,
    order, rising, falling, stash, queue, gain, bias, buckets, w_hbm, wo,
    moved, table,
    w, w_sem, normed, saved, flat_down, acc, total, sums, cur, part, near, away, far, share,
    near_send, near_recv, far_send, far_recv,
    lift_send, lift_recv, gather_send, gather_recv, pass_send, pass_recv,
):
    section = lax.axis_index("section")
    head = lax.axis_index("head")
    chip, core = head // 2, lax.rem(head, 2)
    twin = chip * 2 + (1 - core)
    rows, width = flat_down.shape
    scale = head_dim ** (-0.5)
    span = pair * head_dim

    def peer(k):
        return lax.rem(chip + k, chips)

    def remote(src, dst, send, recv, target):
        return pltpu.make_async_remote_copy(
            src_ref=src, dst_ref=dst, send_sem=send, recv_sem=recv,
            device_id=target, device_id_type=MESH,
        )

    def flat(x):
        return x.astype(jnp.float32).reshape(rows, width)

    def in_block(step, c):
        return w[step, c]

    def load(step, c):
        source = w_hbm.at[:, pl.ds(pl.multiple_of((c * steps + step) * span, 128), span)]
        return pltpu.make_async_copy(source, w.at[step, c], w_sem.at[step, c])

    def out_block(step):
        return wo[pl.ds(pl.multiple_of(step * span, 128), span), :]

    def near_copy(which, t, k):
        return remote(
            part.at[which, t, peer(k), 1 - core], near.at[which, t, k],
            near_send.at[which, t, k], near_recv.at[which, t, k], {"head": twin},
        )

    def far_copy(which, t, k):
        return remote(
            away.at[which, t, k - 1], far.at[which, t, k - 1],
            far_send.at[which, t, k - 1], far_recv.at[which, t, k - 1],
            {"head": peer(k) * 2 + core},
        )

    def lift_copy(which, t, target):
        return remote(
            share.at[which, t], cur.at[which, t + 1, chip, core],
            lift_send.at[which, t], lift_recv.at[which, t], {"section": target},
        )

    def gather_copy(which, t, k):
        rows_here = cur.at[which, t + 1, chip, core]
        return remote(
            rows_here, rows_here,
            gather_send.at[which, t, k - 1], gather_recv.at[which, t, k - 1],
            {"head": peer(k) * 2 + core},
        )

    def pass_copy(which, t, k):
        rows_here = cur.at[which, t + 1, lax.rem(chip - k + chips, chips), core]
        return remote(
            rows_here, rows_here,
            pass_send.at[which, t, k], pass_recv.at[which, t, k], {"head": twin},
        )

    def begin(which, t):
        part[which, t] = acc[...].reshape(part.shape[2:]).astype(jnp.bfloat16)
        for k in list(range(1, chips)) + [0]:
            near_copy(which, t, k).start()

    def fold(which, t):
        for k in range(1, chips):
            near_copy(which, t, k).wait_recv()
            away[which, t, k - 1] = (
                part[which, t, peer(k), core].astype(jnp.float32)
                + near[which, t, k].astype(jnp.float32)
            ).astype(jnp.bfloat16)
            far_copy(which, t, k).start()

    def ends(which):
        if which == 0:
            return section < sections - 1, section + 1, section > 0, section - 1
        return section > 0, section - 1, section < sections - 1, section + 1

    def finish(which, t):
        near_copy(which, t, 0).wait_recv()
        own = part[which, t, chip, core].astype(jnp.float32) + near[which, t, 0].astype(
            jnp.float32
        )
        for k in range(1, chips):
            far_copy(which, t, k).wait_recv()
            own = own + far[which, t, k - 1].astype(jnp.float32)
        before = cur[which, t, chip, core].astype(jnp.float32)
        if which == 0:
            result = before + own
        else:
            x = stash[t, chip, core].astype(jnp.float32)
            inverse = inverse_rms(x)
            cubed = inverse * inverse * inverse
            weighted = gain[...] * own
            result = (
                before
                + inverse * weighted
                - x * cubed * jnp.mean(x * weighted, axis=-1, keepdims=True)
            )
        share[which, t] = result.astype(jnp.bfloat16)
        sends, target, receives, _ = ends(which)

        if t == ticks - 1:
            cur[which, t + 1, chip, core] = result.astype(jnp.bfloat16)
            return

        @pl.when(sends)
        def _():
            lift_copy(which, t, target).start()

        @pl.when(jnp.logical_not(receives))
        def _():
            if which == 0:
                cur[which, t + 1, chip, core] = queue[order[t], chip, core]
            else:
                cur[which, t + 1, chip, core] = share[0, t]

    def spread(which, t):
        sends, target, receives, source = ends(which)

        if t < ticks - 1:
            @pl.when(receives)
            def _():
                lift_copy(which, t, source).wait_recv()

        for k in range(1, chips):
            gather_copy(which, t, k).start()
        pass_copy(which, t, 0).start()

    def relay(which, t):
        for k in range(1, chips):
            gather_copy(which, t, k).wait_recv()
            pass_copy(which, t, k).start()

    def settle(which, t):
        sends, target, receives, source = ends(which)
        for k in range(chips):
            pass_copy(which, t, k).wait_recv()
        for k in range(chips):
            near_copy(which, t, k).wait_send()
            pass_copy(which, t, k).wait_send()
        for k in range(1, chips):
            far_copy(which, t, k).wait_send()
            gather_copy(which, t, k).wait_send()

        if t < ticks - 1:
            @pl.when(sends)
            def _():
                lift_copy(which, t, target).wait_send()

    stages = ((fold, 1), (finish, 3), (spread, 5), (relay, 7))

    def normalize(place, x):
        normed[place * rows : (place + 1) * rows, :] = (
            x * inverse_rms(x) * gain[...]
        ).astype(jnp.bfloat16)

    def project(step, count):
        source = normed[: count * rows, :]
        return [mm(source, in_block(step, c), NN).astype(jnp.bfloat16) for c in range(3)]

    def advance(step, which, t):
        for stage, at in stages:
            @pl.when(step == at * steps // 8)
            def _(stage=stage):
                stage(which, t)

    def forward(t):
        def run(step, carry):
            if t > 0:
                advance(step, 1, t - 1)
            if t == 0:
                for c in range(3):
                    load(step, c).wait()
            qkv = project(step, 1 if t > 0 else ticks + 1)
            if t == 0:
                for c in range(3):
                    saved[step, c] = qkv[c][rows:]
            attended = []
            for h in range(pair):
                q, k, v = (a[:rows, h * head_dim : (h + 1) * head_dim] for a in qkv)
                probs = probabilities(q, k, bias[step * pair + h], scale).astype(jnp.bfloat16)
                attended.append(mm(probs, v, NN).astype(jnp.bfloat16))
            acc[...] += mm(jnp.concatenate(attended, axis=1), out_block(step), NN)
            return carry

        lax.fori_loop(0, steps, run, 0)

    def backward(t):
        def run(step, carry):
            advance(step, 0, t)
            grad_flat = mm(flat_down[...], out_block(step), NT).astype(jnp.bfloat16)
            stacked = []
            for h in range(pair):
                columns = slice(h * head_dim, (h + 1) * head_dim)
                q, k, v = (
                    saved[step, c, t * rows : (t + 1) * rows, columns] for c in range(3)
                )
                g = grad_flat[:, columns]
                probs = probabilities(q, k, bias[step * pair + h], scale)
                grad_probs = mm(g, v, NT)
                grad_value = mm(probs.astype(jnp.bfloat16), g, TN).astype(jnp.bfloat16)
                grad_scores = probs * (
                    grad_probs - jnp.sum(probs * grad_probs, axis=-1, keepdims=True)
                )
                half = grad_scores.astype(jnp.bfloat16)
                grad_query = (mm(half, k, NN) * scale).astype(jnp.bfloat16)
                grad_key = (mm(half, q, TN) * scale).astype(jnp.bfloat16)
                stacked.append((grad_query, grad_key, grad_value))
                if t == 0:
                    total[step * pair + h] = grad_scores
                else:
                    total[step * pair + h] += grad_scores
            back = [
                mm(jnp.concatenate(g, axis=1), in_block(step, c), NT)
                for c, g in enumerate(zip(*stacked))
            ]
            acc[...] += back[0] + back[1] + back[2]
            return carry

        lax.fori_loop(0, steps, run, 0)

    def tables(low, high):
        def run(b, carry):
            chosen = buckets[...] == b
            sums[b] = jnp.concatenate(
                [
                    jnp.sum(jnp.where(chosen, total[h], 0.0), axis=0, keepdims=True)
                    for h in range(total.shape[0])
                ],
                axis=0,
            )
            return carry

        lax.fori_loop(low, high, run, 0)

    for step in range(steps):
        for c in range(3):
            load(step, c).start()
    barrier = pltpu.get_barrier_semaphore()
    greeted = [twin] + [peer(k) * 2 + core for k in range(1, chips)]
    for other in greeted:
        pl.semaphore_signal(barrier, inc=1, device_id={"head": other}, device_id_type=MESH)

    @pl.when(section > 0)
    def _():
        pl.semaphore_signal(
            barrier, inc=1, device_id={"section": section - 1}, device_id_type=MESH
        )

    @pl.when(section < sections - 1)
    def _():
        pl.semaphore_signal(
            barrier, inc=1, device_id={"section": section + 1}, device_id_type=MESH
        )

    cur[0, 0] = rising[...]
    cur[1, 0] = falling[...]
    flat_down[...] = flat(falling[...]).astype(jnp.bfloat16)
    normalize(0, flat(rising[...]))
    for t in range(ticks):
        normalize(t + 1, flat(stash[t]))
    pl.semaphore_wait(
        barrier,
        len(greeted)
        + (section > 0).astype(jnp.int32)
        + (section < sections - 1).astype(jnp.int32),
    )
    for t in range(ticks):
        if t > 0:
            settle(0, t - 1)
            normalize(0, flat(cur[0, t]))
        acc[...] = jnp.zeros_like(acc)
        forward(t)
        begin(0, t)
        if t > 0:
            settle(1, t - 1)
            flat_down[...] = flat(cur[1, t]).astype(jnp.bfloat16)
        acc[...] = jnp.zeros_like(acc)
        backward(t)
        begin(1, t)
    last = ticks - 1
    settle(0, last)
    moved[0] = cur[0, ticks]
    count = sums.shape[0]
    for i, (stage, _at) in enumerate(stages):
        tables(i * count // 4, (i + 1) * count // 4)
        stage(1, last)
    table[...] = jnp.sum(sums[...], axis=-1)
    settle(1, last)
    moved[1] = cur[1, ticks]


def per_device(rising, falling, stash, queue, order, buckets, bias_table, gain, w_qkv, w_out):
    sections = lax.axis_size("section")
    head_count = lax.axis_size("head")
    ticks = stash.shape[1]
    rows, width = rising.shape[1:]
    heads, head_dim = w_qkv.shape[2], w_qkv.shape[4]
    chips, part_rows = head_count // 2, rows // head_count
    pair = 2 if heads % 2 == 0 else 1
    steps, span = heads // pair, pair * head_dim
    others = max(chips - 1, 1)
    w_in = jnp.swapaxes(w_qkv[0], 1, 2).reshape(width, 3 * heads * head_dim)
    w_back = w_out[0].reshape(heads * head_dim, width)
    bucket_ids = jnp.arange(bias_table.shape[1], dtype=jnp.int32)
    onehot = (buckets[None, :, :] == bucket_ids[:, None, None]).astype(jnp.float32)
    biases = jnp.einsum("bij,bh->hij", onehot, bias_table[0], precision=lax.Precision.HIGHEST)
    split = lambda a: a.reshape(a.shape[:-2] + (chips, 2, part_rows, width))
    vmem = pl.BlockSpec(memory_space=pltpu.VMEM)
    tile = (part_rows, width)
    bf16 = lambda *shape: pltpu.VMEM(shape, jnp.bfloat16)
    dma = lambda *shape: pltpu.SemaphoreType.DMA(shape)
    moved, table = pl.pallas_call(
        functools.partial(wave_kernel, ticks, steps, pair, head_dim, chips, sections),
        in_specs=[pl.BlockSpec(memory_space=pltpu.SMEM)] + [vmem] * 7 + [pl.BlockSpec(memory_space=pl.ANY), vmem],
        out_specs=[vmem] * 2,
        out_shape=[
            jax.ShapeDtypeStruct((2, chips, 2) + tile, jnp.bfloat16),
            jax.ShapeDtypeStruct((bias_table.shape[1], heads), jnp.float32),
        ],
        scratch_shapes=[
            bf16(steps, 3, width, span),
            dma(steps, 3),
            bf16((ticks + 1) * rows, width),
            bf16(steps, 3, ticks * rows, span),
            bf16(rows, width),
            pltpu.VMEM((rows, width), jnp.float32),
            pltpu.VMEM((heads, rows, rows), jnp.float32),
            pltpu.VMEM((bias_table.shape[1], heads, rows), jnp.float32),
            bf16(2, ticks + 1, chips, 2, *tile),
            bf16(2, ticks, chips, 2, *tile),
            bf16(2, ticks, chips, *tile),
            bf16(2, ticks, others, *tile),
            bf16(2, ticks, others, *tile),
            bf16(2, ticks, *tile),
            dma(2, ticks, chips), dma(2, ticks, chips),
            dma(2, ticks, others), dma(2, ticks, others),
            dma(2, ticks), dma(2, ticks),
            dma(2, ticks, others), dma(2, ticks, others),
            dma(2, ticks, chips), dma(2, ticks, chips),
        ],
        compiler_params=pltpu.CompilerParams(
            collective_id=0, has_side_effects=True, vmem_limit_bytes=40 << 20
        ),
    )(
        order, split(rising[0]), split(falling[0]), split(stash[0]), split(queue), gain,
        biases, buckets, w_in, w_back,
    )
    moved = moved.reshape(2, 1, rows, width)
    return (moved[0], moved[1], table[None])


def solution(mesh):
    return jax.shard_map(
        per_device,
        mesh=mesh,
        in_specs=(
            P(("groups", "section"), None, None),
            P(("groups", "section"), None, None),
            P(("groups", "section"), None, None, None),
            P("groups", None, None),
            P("groups"),
            P(),
            P("section", None, "head"),
            P("section", None),
            P("section", None, "head", None, None),
            P("section", "head", None, None),
        ),
        out_specs=(
            P(("groups", "section"), None, None),
            P(("groups", "section"), None, None),
            P(("groups", "section"), None, "head"),
        ),
        check_vma=False,
    )
```

time: 137 us -> 118 us (0.86)
  Pallas kernels: 112 us -> 99.3 us
  matrix products: 4.95 us -> 1.59 us
  local copies, waits for them, and re-layouts: 18.8 us -> 16.6 us
    pallas_call x1, Pallas kernels: 112 us -> 99.3 us  [per_device(): pl.pallas_call(functools.partial(wave_kernel, ticks, steps, pair, head_di...]
    dot_general x1 -> x0, matrix products: 3.37 us -> none  [per_device(): jnp.einsum('bij,hij->bh', onehot, total, precision=lax.Precision.HIGHEST)]
    unnamed x7 -> x20, local copies, waits for them, and re-layouts: 17.5 us -> 15.4 us
where the time goes in v1:
time: 118 us
  Pallas kernels  99.3 us (84%)
  local copies, waits for them, and re-layouts  16.6 us (14%)
  matrix products  1.59 us (1%)
    pallas_call x1, Pallas kernels, per_device(): pl.pallas_call(functools.partial(wave_kernel, ticks, steps, pair, head_di...  99.3 us
    unnamed x20, local copies, waits for them, and re-layouts  15.4 us

profile of v1, /device:TPU:0, one launch (start us, length us, event | category | flops | bytes accessed | tf_op | source)
XLA Modules:
  0.0 118.2 jit_solution(9195907186546218680)
XLA Ops:
  0.6 0.0 copy-start
  0.6 0.7 copy-done
  1.3 1.6 %fusion = f32[128,128,16]{1,2,0:T(8,128)S(1)} fusion(s32[128,128]{1,0:T(8,128)} %buckets.1, f32[1,32,16]{1,2,0:T(8,128)S(1)} %copy-done), kind=kOutput, calls=%fused_computation.2 | convolution fusion | flops 101187584 | bytes 1116160 | tf_op jit(solution)/shard_map/bij,bh->hij/dot_general | solution.py:352
  2.9 0.3 copy.19
  3.3 0.0 copy-start.1
  3.3 0.0 copy-start.2
  3.3 0.0 copy-start.3
  3.3 0.0 copy-start.4
  3.3 0.0 copy-start.5
  3.3 0.0 copy-start.6
  3.3 0.0 copy-start.7
  3.4 0.0 copy-start.8
  3.4 14.0 %copy.18 = bf16[128,8,48,128]{3,1,2,0:T(8,128)(2,1)} copy(bf16[128,8,48,128]{3,2,1,0:T(8,128)(2,1)} %bitcast.31) | data formatting | bytes 25165824
  17.4 0.0 copy-done.1
  17.4 0.0 copy-done.2
  17.4 0.0 copy-done.3
  17.4 0.0 copy-done.4
  17.4 0.0 copy-done.5
  17.4 0.0 copy-done.6
  17.4 0.0 copy-done.7
  17.4 0.0 copy-done.8
  17.4 99.3 %shard_map.121 = (bf16[2,2,2,32,1024]{4,3,2,1,0:T(8,128)(2,1)S(1)}, f32[32,16]{1,0:T(8,128)S(1)}) custom-call(s32[6]{0:T(128)S(1)} %copy-done.8, bf16[2,2,32,1024]{3,2,1,0:T(8,128)(2,1)S(1)} %bitcast.27, bf16[2,2,32,1024]{3,2,1,0:T(8,128)(2,1)S(1)} %bitcast.28, bf16[3,2,2,32,1024]{4,3,2,1,0:T(8,128)(2,1)S(1)} %bitcast.26, ...), custom_call_target="tpu_custom_call" | custom-call | tf_op jit(solution)/shard_map/pallas_call | solution.py:358
  116.7 0.7 copy.14
  117.4 0.8 fusion.3
Async XLA Ops:
  0.6 0.7 copy-start
  3.3 14.1 %copy-start.1 = (bf16[1,16,128,1024]{3,2,1,0:T(8,128)(2,1)S(1)}, bf16[1,16,128,1024]{3,2,1,0:T(8,128)(2,1)}, u32[]{:S(2)}) copy-start(bf16[1,16,128,1024]{3,2,1,0:T(8,128)(2,1)} %param.19) | copy-start | bytes 12582916
  3.3 14.1 %copy-start.2 = (bf16[6,128,1024]{2,1,0:T(8,128)(2,1)S(1)}, bf16[6,128,1024]{2,1,0:T(8,128)(2,1)}, u32[]{:S(2)}) copy-start(bf16[6,128,1024]{2,1,0:T(8,128)(2,1)} %param.13) | copy-start | bytes 4718596
  3.3 14.1 %copy-start.3 = (bf16[1,3,128,1024]{3,2,1,0:T(8,128)(2,1)S(1)}, bf16[1,3,128,1024]{3,2,1,0:T(8,128)(2,1)}, u32[]{:S(2)}) copy-start(bf16[1,3,128,1024]{3,2,1,0:T(8,128)(2,1)} %param.12) | copy-start | bytes 2359300
  3.3 14.1 %copy-start.4 = (bf16[1,128,1024]{2,1,0:T(8,128)(2,1)S(1)}, bf16[1,128,1024]{2,1,0:T(8,128)(2,1)}, u32[]{:S(2)}) copy-start(bf16[1,128,1024]{2,1,0:T(8,128)(2,1)} %param.10) | copy-start | bytes 786436
  3.3 14.1 %copy-start.5 = (bf16[1,128,1024]{2,1,0:T(8,128)(2,1)S(1)}, bf16[1,128,1024]{2,1,0:T(8,128)(2,1)}, u32[]{:S(2)}) copy-start(bf16[1,128,1024]{2,1,0:T(8,128)(2,1)} %param.11) | copy-start | bytes 786436
  3.3 14.1 %copy-start.6 = (s32[128,128]{1,0:T(8,128)S(1)}, s32[128,128]{1,0:T(8,128)}, u32[]{:S(2)}) copy-start(s32[128,128]{1,0:T(8,128)} %buckets.1) | copy-start | bytes 196612
  3.3 14.1 %copy-start.7 = (f32[1,1024]{1,0:T(1,128)S(1)}, f32[1,1024]{1,0:T(1,128)}, u32[]{:S(2)}) copy-start(f32[1,1024]{1,0:T(1,128)} %gain.1) | copy-start | bytes 12292
  3.4 14.1 %copy-start.8 = (s32[6]{0:T(128)S(1)}, s32[6]{0:T(128)}, u32[]{:S(2)}) copy-start(s32[6]{0:T(128)} %order.1) | copy-start | bytes 76

commit v2 on v1

--- a/solution.py
+++ b/solution.py
@@ -178,6 +178,7 @@
 
     def settle(which, t):
         sends, target, receives, source = ends(which)
+        relay(which, t)
         for k in range(chips):
             pass_copy(which, t, k).wait_recv()
         for k in range(chips):
@@ -192,7 +193,7 @@
             def _():
                 lift_copy(which, t, target).wait_send()
 
-    stages = ((fold, 1), (finish, 3), (spread, 5), (relay, 7))
+    stages = ((fold, 2), (finish, 4), (spread, 6))
 
     def normalize(place, x):
         normed[place * rows : (place + 1) * rows, :] = (
@@ -328,7 +329,7 @@
     moved[0] = cur[0, ticks]
     count = sums.shape[0]
     for i, (stage, _at) in enumerate(stages):
-        tables(i * count // 4, (i + 1) * count // 4)
+        tables(i * count // 3, (i + 1) * count // 3)
         stage(1, last)
     table[...] = jnp.sum(sums[...], axis=-1)
     settle(1, last)
@@ -342,7 +343,7 @@
     rows, width = rising.shape[1:]
     heads, head_dim = w_qkv.shape[2], w_qkv.shape[4]
     chips, part_rows = head_count // 2, rows // head_count
-    pair = 2 if heads % 2 == 0 else 1
+    pair = next(p for p in (4, 4, 2, 1) if heads % p == 0)
     steps, span = heads // pair, pair * head_dim
     others = max(chips - 1, 1)
     w_in = jnp.swapaxes(w_qkv[0], 1, 2).reshape(width, 3 * heads * head_dim)

time: 118 us -> 116 us (0.983)
  Pallas kernels: 99.3 us -> 96.4 us
    pallas_call x1, Pallas kernels: 99.3 us -> 96.4 us  [per_device(): pl.pallas_call(functools.partial(wave_kernel, ticks, steps, pair, head_di...]
where the time goes in v2:
time: 116 us; the launch traced here: 115 us
  Pallas kernels  96.4 us (83%)
  local copies, waits for them, and re-layouts  16.6 us (14%)
  matrix products  1.59 us (1%)
    pallas_call x1, Pallas kernels, per_device(): pl.pallas_call(functools.partial(wave_kernel, ticks, steps, pair, head_di...  96.4 us
    unnamed x20, local copies, waits for them, and re-layouts  15.4 us

profile of v2, /device:TPU:0, one launch (start us, length us, event | category | flops | bytes accessed | tf_op | source)
XLA Modules:
  0.0 115.3 jit_solution(2983665819503673934)
XLA Ops:
  0.6 0.0 copy-start
  0.6 0.7 copy-done
  1.3 1.6 %fusion = f32[128,128,16]{1,2,0:T(8,128)S(1)} fusion(s32[128,128]{1,0:T(8,128)} %buckets.1, f32[1,32,16]{1,2,0:T(8,128)S(1)} %copy-done), kind=kOutput, calls=%fused_computation.2 | convolution fusion | flops 101187584 | bytes 1116160 | tf_op jit(solution)/shard_map/bij,bh->hij/dot_general | solution.py:353
  2.9 0.3 copy.19
  3.3 0.0 copy-start.1
  3.3 0.0 copy-start.2
  3.3 0.0 copy-start.3
  3.3 0.0 copy-start.4
  3.3 0.0 copy-start.5
  3.3 0.0 copy-start.6
  3.3 0.0 copy-start.7
  3.4 0.0 copy-start.8
  3.4 14.0 %copy.18 = bf16[128,8,48,128]{3,1,2,0:T(8,128)(2,1)} copy(bf16[128,8,48,128]{3,2,1,0:T(8,128)(2,1)} %bitcast.31) | data formatting | bytes 25165824
  17.4 0.0 copy-done.1
  17.4 0.0 copy-done.2
  17.4 0.0 copy-done.3
  17.4 0.0 copy-done.4
  17.4 0.0 copy-done.5
  17.4 0.0 copy-done.6
  17.4 0.0 copy-done.7
  17.4 0.0 copy-done.8
  17.4 96.4 %shard_map.121 = (bf16[2,2,2,32,1024]{4,3,2,1,0:T(8,128)(2,1)S(1)}, f32[32,16]{1,0:T(8,128)S(1)}) custom-call(s32[6]{0:T(128)S(1)} %copy-done.8, bf16[2,2,32,1024]{3,2,1,0:T(8,128)(2,1)S(1)} %bitcast.27, bf16[2,2,32,1024]{3,2,1,0:T(8,128)(2,1)S(1)} %bitcast.28, bf16[3,2,2,32,1024]{4,3,2,1,0:T(8,128)(2,1)S(1)} %bitcast.26, ...), custom_call_target="tpu_custom_call" | custom-call | tf_op jit(solution)/shard_map/pallas_call | solution.py:359
  113.8 0.7 copy.14
  114.5 0.8 fusion.3
Async XLA Ops:
  0.6 0.7 copy-start
  3.3 14.1 %copy-start.1 = (bf16[1,16,128,1024]{3,2,1,0:T(8,128)(2,1)S(1)}, bf16[1,16,128,1024]{3,2,1,0:T(8,128)(2,1)}, u32[]{:S(2)}) copy-start(bf16[1,16,128,1024]{3,2,1,0:T(8,128)(2,1)} %param.19) | copy-start | bytes 12582916
  3.3 14.1 %copy-start.2 = (bf16[6,128,1024]{2,1,0:T(8,128)(2,1)S(1)}, bf16[6,128,1024]{2,1,0:T(8,128)(2,1)}, u32[]{:S(2)}) copy-start(bf16[6,128,1024]{2,1,0:T(8,128)(2,1)} %param.13) | copy-start | bytes 4718596
  3.3 14.1 %copy-start.3 = (bf16[1,3,128,1024]{3,2,1,0:T(8,128)(2,1)S(1)}, bf16[1,3,128,1024]{3,2,1,0:T(8,128)(2,1)}, u32[]{:S(2)}) copy-start(bf16[1,3,128,1024]{3,2,1,0:T(8,128)(2,1)} %param.12) | copy-start | bytes 2359300
  3.3 14.1 %copy-start.4 = (bf16[1,128,1024]{2,1,0:T(8,128)(2,1)S(1)}, bf16[1,128,1024]{2,1,0:T(8,128)(2,1)}, u32[]{:S(2)}) copy-start(bf16[1,128,1024]{2,1,0:T(8,128)(2,1)} %param.10) | copy-start | bytes 786436
  3.3 14.1 %copy-start.5 = (bf16[1,128,1024]{2,1,0:T(8,128)(2,1)S(1)}, bf16[1,128,1024]{2,1,0:T(8,128)(2,1)}, u32[]{:S(2)}) copy-start(bf16[1,128,1024]{2,1,0:T(8,128)(2,1)} %param.11) | copy-start | bytes 786436
  3.3 14.1 %copy-start.6 = (s32[128,128]{1,0:T(8,128)S(1)}, s32[128,128]{1,0:T(8,128)}, u32[]{:S(2)}) copy-start(s32[128,128]{1,0:T(8,128)} %buckets.1) | copy-start | bytes 196612
  3.3 14.1 %copy-start.7 = (f32[1,1024]{1,0:T(1,128)S(1)}, f32[1,1024]{1,0:T(1,128)}, u32[]{:S(2)}) copy-start(f32[1,1024]{1,0:T(1,128)} %gain.1) | copy-start | bytes 12292
  3.4 14.1 %copy-start.8 = (s32[6]{0:T(128)S(1)}, s32[6]{0:T(128)}, u32[]{:S(2)}) copy-start(s32[6]{0:T(128)} %order.1) | copy-start | bytes 76
